TPU v7x, 256 devices: a whole 4x4x8 slice. The times are simulated.
256 devices in a mesh: seq: 16 (over y, x), dp: 16 (over z, core).
Axes of the slice: x: 4, y: 4, z: 8, core: 2. Of those that a mesh axis runs over, the one named last changes fastest.
Arguments:
- queries: bfloat16 [128, 256, 4096], P(None, ('seq', 'dp')), may hold values from -8 to 8
- keys_in: bfloat16 [128, 256, 4096], P(None, ('seq', 'dp')), may hold values from -8 to 8
- values: bfloat16 [128, 256, 4096], P(None, ('seq', 'dp')), may hold values from -6 to 6
- grad_out: bfloat16 [10, 4096, 4096], P(None, ('seq', 'dp')), may hold values from -6 to 6
- doc_lengths: int32 [24], replicated, may hold values from 1 to 2560, as said below
- doc_group: int32 [24], replicated, may hold values from 0 to 15, as said below
Outputs:
- attended: bfloat16 [10, 4096, 4096], P(None, ('seq', 'dp'))
- grad_queries: bfloat16 [128, 256, 4096], P(None, ('seq', 'dp'))
- grad_keys: bfloat16 [128, 256, 4096], P(None, ('seq', 'dp'))
- grad_values: bfloat16 [128, 256, 4096], P(None, ('seq', 'dp'))
Inputs may be any that keep to these rules, and one draw needn't show every extreme that they name: `doc_lengths`: the documents lie one after another in the packed batch in index order and their lengths sum to 32768. The documents of one group are consecutive, groups in increasing order; every group holds a whole multiple of 256 tokens, at most 2560, and some group holds exactly that many. `doc_group`: never falls from one document to the next; every group takes at least one document.
All inputs are finite; a program needn't handle non-finite values.
Results may differ from a plain program's by a relative error of at most 0.02.
Values may be sent and summed in bfloat16 or wider, within the bound.
A program may use at most 64 MiB of HBM per device.

v0:
```python
import jax
import jax.numpy as jnp
import numpy as np
from jax import lax
from jax.sharding import PartitionSpec as P

HEAD = 128
NEGATIVE_FILL = -1e30


def group_tables(doc_lengths, doc_group, group_count, per_unit):
    doc_ends = jnp.cumsum(doc_lengths)
    member = (doc_group[:, None] == jnp.arange(group_count, dtype=jnp.int32)[None, :]).astype(
        jnp.int32
    )
    group_units = jnp.sum(member * doc_lengths[:, None], axis=0) // per_unit
    first_unit = jnp.cumsum(group_units) - group_units
    return (doc_ends, group_units, first_unit)


def attend_group(
    head_q, head_k, head_v, head_do, token_ids, doc_query, doc_key, row_live, block_rows
):
    row_count, head_count, head_dim = head_q.shape
    blocks = row_count // block_rows
    score_scale = head_dim ** (-0.5)
    later, earlier = np.tril_indices(blocks)
    query_block = jnp.asarray(later, dtype=jnp.int32)
    key_block = jnp.asarray(earlier, dtype=jnp.int32)
    pair_total = int(later.shape[0])
    block_docs = doc_query.reshape(blocks, block_rows)
    live_blocks = row_live.reshape(blocks, block_rows)
    lowest = jnp.min(jnp.where(live_blocks, block_docs, 1 << 30), axis=1)
    highest = jnp.max(jnp.where(live_blocks, block_docs, -1), axis=1)
    needed = (
        (highest[key_block] >= lowest[query_block])
        & (lowest[key_block] <= highest[key_block])
        & (lowest[query_block] <= highest[query_block])
    )

    def tile_scores(pair_index):
        q_start = query_block[pair_index] * block_rows
        k_start = key_block[pair_index] * block_rows
        q_rows = lax.dynamic_slice_in_dim(head_q, q_start, block_rows, 0)
        k_rows = lax.dynamic_slice_in_dim(head_k, k_start, block_rows, 0)
        same_doc = (
            lax.dynamic_slice_in_dim(doc_query, q_start, block_rows, 0)[:, None]
            == lax.dynamic_slice_in_dim(doc_key, k_start, block_rows, 0)[None, :]
        )
        earlier_key = (
            lax.dynamic_slice_in_dim(token_ids, k_start, block_rows, 0)[None, :]
            <= lax.dynamic_slice_in_dim(token_ids, q_start, block_rows, 0)[:, None]
        )
        scores = (
            jnp.einsum("qhe,khe->qhk", q_rows, k_rows, preferred_element_type=jnp.float32)
            * score_scale
        )
        return (q_start, k_start, q_rows, k_rows, scores, (same_doc & earlier_key)[:, None, :])

    def stats_step(pair_index, loop_state):

        def stats_compute(inner_state):
            row_top, row_total = inner_state
            q_start, k_start, q_rows, k_rows, scores, allowed = tile_scores(pair_index)
            old_top = lax.dynamic_slice_in_dim(row_top, q_start, block_rows, 0)
            old_total = lax.dynamic_slice_in_dim(row_total, q_start, block_rows, 0)
            new_top = jnp.maximum(
                old_top, jnp.max(jnp.where(allowed, scores, NEGATIVE_FILL), axis=2)
            )
            exp_terms = jnp.sum(
                jnp.where(allowed, jnp.exp(scores - new_top[:, :, None]), 0.0), axis=2
            )
            new_total = old_total * jnp.exp(old_top - new_top) + exp_terms
            return (
                lax.dynamic_update_slice_in_dim(row_top, new_top, q_start, 0),
                lax.dynamic_update_slice_in_dim(row_total, new_total, q_start, 0),
            )

        return lax.cond(needed[pair_index], stats_compute, lambda unchanged: unchanged, loop_state)

    start_state = (
        jnp.full((row_count, head_count), NEGATIVE_FILL, jnp.float32),
        jnp.zeros((row_count, head_count), jnp.float32),
    )
    row_top, row_total = lax.fori_loop(0, pair_total, stats_step, start_state)
    log_total = jnp.where(row_live[:, None], row_top + jnp.log(row_total), 0.0)

    def value_step(pair_index, accumulated):

        def value_compute(inner_state):
            q_start, k_start, q_rows, k_rows, scores, allowed = tile_scores(pair_index)
            row_log = lax.dynamic_slice_in_dim(log_total, q_start, block_rows, 0)
            weight = jnp.where(allowed, jnp.exp(scores - row_log[:, :, None]), 0.0).astype(
                jnp.bfloat16
            )
            v_rows = lax.dynamic_slice_in_dim(head_v, k_start, block_rows, 0)
            part_sum = jnp.einsum(
                "qhk,khe->qhe", weight, v_rows, preferred_element_type=jnp.float32
            )
            current = lax.dynamic_slice_in_dim(inner_state, q_start, block_rows, 0)
            return lax.dynamic_update_slice_in_dim(inner_state, current + part_sum, q_start, 0)

        return lax.cond(needed[pair_index], value_compute, lambda unchanged: unchanged, accumulated)

    accumulated = lax.fori_loop(
        0, pair_total, value_step, jnp.zeros((row_count, head_count, head_dim), jnp.float32)
    )
    attended = accumulated.astype(jnp.bfloat16)
    delta_all = jnp.sum(head_do.astype(jnp.float32) * attended.astype(jnp.float32), axis=2)

    def grad_step(pair_index, loop_state):

        def grad_compute(inner_state):
            grad_q, grad_k, grad_v = inner_state
            q_start, k_start, q_rows, k_rows, scores, allowed = tile_scores(pair_index)
            row_log = lax.dynamic_slice_in_dim(log_total, q_start, block_rows, 0)
            row_delta = lax.dynamic_slice_in_dim(delta_all, q_start, block_rows, 0)
            weight_full = jnp.where(allowed, jnp.exp(scores - row_log[:, :, None]), 0.0)
            do_rows = lax.dynamic_slice_in_dim(head_do, q_start, block_rows, 0)
            v_rows = lax.dynamic_slice_in_dim(head_v, k_start, block_rows, 0)
            grad_prob = jnp.einsum(
                "qhe,khe->qhk", do_rows, v_rows, preferred_element_type=jnp.float32
            )
            grad_score = (weight_full * (grad_prob - row_delta[:, :, None])).astype(jnp.bfloat16)
            add_values = jnp.einsum(
                "qhk,qhe->khe",
                weight_full.astype(jnp.bfloat16),
                do_rows,
                preferred_element_type=jnp.float32,
            )
            add_queries = jnp.einsum(
                "qhk,khe->qhe", grad_score, k_rows, preferred_element_type=jnp.float32
            )
            add_keys = jnp.einsum(
                "qhk,qhe->khe", grad_score, q_rows, preferred_element_type=jnp.float32
            )
            grad_q = lax.dynamic_update_slice_in_dim(
                grad_q,
                lax.dynamic_slice_in_dim(grad_q, q_start, block_rows, 0) + add_queries,
                q_start,
                0,
            )
            grad_k = lax.dynamic_update_slice_in_dim(
                grad_k,
                lax.dynamic_slice_in_dim(grad_k, k_start, block_rows, 0) + add_keys,
                k_start,
                0,
            )
            grad_v = lax.dynamic_update_slice_in_dim(
                grad_v,
                lax.dynamic_slice_in_dim(grad_v, k_start, block_rows, 0) + add_values,
                k_start,
                0,
            )
            return (grad_q, grad_k, grad_v)

        return lax.cond(needed[pair_index], grad_compute, lambda unchanged: unchanged, loop_state)

    zero_grads = jnp.zeros((row_count, head_count, head_dim), jnp.float32)
    grad_q, grad_k, grad_v = lax.fori_loop(
        0, pair_total, grad_step, (zero_grads, zero_grads, zero_grads)
    )
    return (
        attended,
        (grad_q * score_scale).astype(jnp.bfloat16),
        (grad_k * score_scale).astype(jnp.bfloat16),
        grad_v.astype(jnp.bfloat16),
    )


def to_groups(first_part, second_part, third_part):
    return (
        lax.all_to_all(first_part, "dp", split_axis=1, concat_axis=1, tiled=True),
        lax.all_to_all(second_part, "dp", split_axis=1, concat_axis=1, tiled=True),
        lax.all_to_all(third_part, "dp", split_axis=1, concat_axis=1, tiled=True),
    )


def to_heads(first_part, second_part, third_part, fourth_part):
    return (
        lax.all_to_all(first_part, "seq", split_axis=2, concat_axis=1, tiled=True),
        lax.all_to_all(second_part, "seq", split_axis=2, concat_axis=1, tiled=True),
        lax.all_to_all(third_part, "seq", split_axis=2, concat_axis=1, tiled=True),
        lax.all_to_all(fourth_part, "seq", split_axis=2, concat_axis=1, tiled=True),
    )


def from_heads(first_part, second_part, third_part, fourth_part):
    return (
        lax.all_to_all(first_part, "seq", split_axis=1, concat_axis=2, tiled=True),
        lax.all_to_all(second_part, "seq", split_axis=1, concat_axis=2, tiled=True),
        lax.all_to_all(third_part, "seq", split_axis=1, concat_axis=2, tiled=True),
        lax.all_to_all(fourth_part, "seq", split_axis=1, concat_axis=2, tiled=True),
    )


def to_packed(first_part, second_part, third_part):
    return (
        lax.all_to_all(first_part, "dp", split_axis=1, concat_axis=1, tiled=True),
        lax.all_to_all(second_part, "dp", split_axis=1, concat_axis=1, tiled=True),
        lax.all_to_all(third_part, "dp", split_axis=1, concat_axis=1, tiled=True),
    )


def body(queries, keys_in, values, grad_out, doc_lengths, doc_group):
    seq_count = lax.axis_size("seq")
    group_count = lax.axis_size("dp")
    devices = seq_count * group_count
    local_rows = queries.shape[0]
    features = queries.shape[2]
    head_dim = HEAD
    local_heads = features // (seq_count * head_dim)
    capacity = grad_out.shape[0]
    doc_ends, group_units, first_unit = group_tables(doc_lengths, doc_group, group_count, devices)
    slot_ids = jnp.arange(capacity, dtype=jnp.int32)[:, None]
    filled = slot_ids < group_units[None, :]
    source_row = jnp.where(filled, first_unit[None, :] + slot_ids, 0).reshape(-1)
    row_ids = jnp.arange(local_rows, dtype=jnp.int32)
    row_group = jnp.sum((first_unit + group_units)[None, :] <= row_ids[:, None], axis=1)
    row_first = jnp.sum(
        jnp.where(
            jnp.arange(group_count, dtype=jnp.int32)[None, :] == row_group[:, None],
            first_unit[None, :],
            0,
        ),
        axis=1,
    )
    target_row = (row_ids - row_first) * group_count + row_group

    def pack_rows(local):
        taken_rows = jnp.take(local, source_row, axis=0).reshape(
            (capacity, group_count) + local.shape[1:]
        )
        keep_mask = filled.reshape((capacity, group_count) + (1,) * (local.ndim - 1))
        return jnp.where(keep_mask, taken_rows, jnp.zeros((), local.dtype))

    def unpack_rows(balanced):
        flat_rows = balanced.reshape((capacity * group_count,) + balanced.shape[2:])
        return jnp.take(flat_rows, target_row, axis=0)

    head_shape = (seq_count, local_heads, head_dim)
    group_rows = capacity * group_count * seq_count
    flat_q = queries.reshape(local_rows, features)
    flat_k = keys_in.reshape(local_rows, features)
    flat_v = values.reshape(local_rows, features)
    cot_rows = grad_out.reshape((capacity * group_count, 1) + head_shape)
    moved_q, moved_k, moved_v = to_groups(pack_rows(flat_q), pack_rows(flat_k), pack_rows(flat_v))
    lead_shape = (capacity * group_count, 1) + head_shape
    head_q, head_k, head_v, head_do = to_heads(
        moved_q.reshape(lead_shape),
        moved_k.reshape(lead_shape),
        moved_v.reshape(lead_shape),
        cot_rows,
    )
    work_shape = (group_rows, local_heads, head_dim)
    head_q = head_q.reshape(work_shape)
    head_k = head_k.reshape(work_shape)
    head_v = head_v.reshape(work_shape)
    head_do = head_do.reshape(work_shape)
    group_index = lax.axis_index("dp")
    slot_axis = jnp.arange(capacity, dtype=jnp.int32)[:, None, None]
    data_axis = jnp.arange(group_count, dtype=jnp.int32)[None, :, None]
    seq_axis = jnp.arange(seq_count, dtype=jnp.int32)[None, None, :]
    token_ids = (
        (first_unit[group_index] + slot_axis) * devices + seq_axis * group_count + data_axis
    ).reshape(-1)
    row_live = jnp.broadcast_to(
        slot_axis < group_units[group_index], (capacity, group_count, seq_count)
    ).reshape(-1)
    doc_of = jnp.sum(doc_ends[None, :] <= token_ids[:, None], axis=1)
    doc_query = jnp.where(row_live, doc_of, -1)
    doc_key = jnp.where(row_live, doc_of, -2)
    divisors = [
        factor
        for factor in range(1, capacity + 1)
        if capacity % factor == 0 and factor * devices <= 512
    ]
    block_rows = divisors[-1] * devices
    attended, grad_q, grad_k, grad_v = attend_group(
        head_q, head_k, head_v, head_do, token_ids, doc_query, doc_key, row_live, block_rows
    )
    back_shape = (capacity * group_count, seq_count, 1, local_heads, head_dim)
    seq_out, seq_q, seq_k, seq_v = from_heads(
        attended.reshape(back_shape),
        grad_q.reshape(back_shape),
        grad_k.reshape(back_shape),
        grad_v.reshape(back_shape),
    )
    flat_shape = (capacity, group_count, features)
    home_q, home_k, home_v = to_packed(
        seq_q.reshape(flat_shape), seq_k.reshape(flat_shape), seq_v.reshape(flat_shape)
    )
    out_q = unpack_rows(home_q)
    out_k = unpack_rows(home_k)
    out_v = unpack_rows(home_v)
    packed_shape = (local_rows, 1, features)
    return (
        seq_out.reshape(capacity, group_count, features),
        out_q.reshape(packed_shape),
        out_k.reshape(packed_shape),
        out_v.reshape(packed_shape),
    )


def solution(mesh):
    return jax.shard_map(
        body,
        mesh=mesh,
        in_specs=(
            P(None, ("seq", "dp"), None),
            P(None, ("seq", "dp"), None),
            P(None, ("seq", "dp"), None),
            P(None, ("seq", "dp"), None),
            P(),
            P(),
        ),
        out_specs=(
            P(None, ("seq", "dp"), None),
            P(None, ("seq", "dp"), None),
            P(None, ("seq", "dp"), None),
            P(None, ("seq", "dp"), None),
        ),
        check_vma=False,
    )
```

profile of v0, /device:TPU:1, one launch (start us, length us, event | category | flops | bytes accessed | tf_op | source)
XLA Modules:
  0.0 1028.3 jit_solution(3317540687620245920)
XLA Ops:
  5.9 7.7 all-to-all-start.7
  25.8 10.6 %copy_select_fusion = (bf16[10,16,4096]{2,0,1:T(8,128)(2,1)S(1)}, bf16[10,16,4096]{2,0,1:T(8,128)(2,1)}, bf16[10,16,4096]{2,0,1:T(8,128)(2,1)}) fusion(bf16[10,16,4096]{2,1,0:T(8,128)(2,1)} %bitcast.152, pred[10,16]{0,1:T(8,128)(4,1)S(1)} %copy.155, bf16[10,16,4096]{2,1,0:T(8,128)(2,1)} %bitcast.153, bf16[10,16,4096]{2,1,0:T(8,128)(2,1)} %bitcast.154), kind=kLoop, calls=%fused_computation.84 | loop fusion | flops 1966080 | bytes 7864480 | tf_op jit(solution)/shard_map/jit(_where)/select_n | solution.py:235
  36.4 60.6 %all_to_all.102 = bf16[10,16,4096]{2,0,1:T(8,128)(2,1)} all-to-all(bf16[10,16,4096]{2,0,1:T(8,128)(2,1)} %get-tuple-element.1227), channel_id=1, replica_groups=mesh['seq'=16,'dp'=16] {'dp'}, dimensions={1} | all-to-all | bytes 2621440 | tf_op jit(solution)/shard_map/all_to_all | solution.py:174
  97.0 53.7 %all_to_all.103 = bf16[10,16,4096]{2,0,1:T(8,128)(2,1)} all-to-all(bf16[10,16,4096]{2,0,1:T(8,128)(2,1)S(1)} %get-tuple-element.1226), channel_id=1, replica_groups=mesh['seq'=16,'dp'=16] {'dp'}, dimensions={1} | all-to-all | bytes 2621440 | tf_op jit(solution)/shard_map/all_to_all | solution.py:173
  165.1 37.7 %all-to-all-done = bf16[10,16,4096]{2,0,1:T(8,128)(2,1)S(1)} async-done(((bf16[10,16,4096]{2,0,1:T(8,128)(2,1)}), bf16[10,16,4096]{2,0,1:T(8,128)(2,1)S(1)}, u32[]{:S(2)}, u32[]{:S(2)}) %all-to-all-start) | async-done | bytes 1310752 | tf_op jit(solution)/shard_map/all_to_all | solution.py:175
  202.8 7.0 all-to-all-start.3
  220.4 9.8 all-to-all-done.3
  243.5 9.0 all-to-all-done.5
  269.4 117.6 %while.54 = (s32[]{:T(128)}, f32[2560,2]{0,1:T(2,128)S(1)}, f32[2560,2]{0,1:T(2,128)S(1)}, pred[15]{0:T(512)(128)(4,1)S(1)}, s32[2560]{0:T(1024)S(1)}, /*index=5...) while((s32[]{:T(128)}, f32[2560,2]{0,1:T(2,128)S(1)}, ...), condition=%wide.region_13.15_spmd.clone.clone, body=%wide.region_8.14_spmd.sunk.clone.clone.sunk | while | flops 138678800 | bytes 5712918 | solution.py:85
  270.7 6.5 conditional.15
  278.5 6.5 conditional.15
  286.3 6.5 conditional.15
  294.2 6.5 conditional.15
  302.0 6.5 conditional.15
  309.8 6.5 conditional.15
  317.7 6.5 conditional.15
  325.5 6.5 conditional.15
  333.4 6.5 conditional.15
  341.2 6.5 conditional.15
  349.0 6.5 conditional.15
  356.9 6.5 conditional.15
  364.7 6.5 conditional.15
  380.4 6.5 conditional.15
  393.6 130.8 %while.55 = (s32[]{:T(128)}, f32[2560,2,128]{0,2,1:T(8,128)}, pred[15]{0:T(512)(128)(4,1)S(1)}, bf16[2560,2,128]{0,2,1:T(8,128)(2,1)}, s32[2560]{0:T(1024)S(1)},...) while((s32[]{:T(128)}, f32[2560,2,128]{0,2,1:T(8,128)}, ...), condition=%wide.region_17.19_spmd.clone.clone, body=%wide.region_14.18_spmd.sunk.clone.clone.sunk | while | flops 271452672 | bytes 2450426 | solution.py:105
  394.9 7.5 conditional.16
  403.6 7.5 conditional.16
  412.4 7.5 conditional.16
  421.2 7.5 conditional.16
  429.9 7.5 conditional.16
  438.6 7.5 conditional.16
  447.4 7.4 conditional.16
  456.1 7.4 conditional.16
  464.8 7.4 conditional.16
  473.4 7.4 conditional.16
  482.1 7.5 conditional.16
  490.8 7.5 conditional.16
  499.5 7.5 conditional.16
  508.3 7.5 conditional.16
  517.0 7.5 conditional.16
  531.5 229.7 %while.56 = (s32[]{:T(128)}, f32[2560,2,128]{0,2,1:T(8,128)}, f32[2560,2,128]{0,2,1:T(8,128)}, f32[2560,2,128]{0,2,1:T(8,128)S(1)}, pred[15]{0:T(512)(128)(4,1)S...) while((s32[]{:T(128)}, f32[2560,2,128]{0,2,1:T(8,128)}, ...), condition=%wide.region_22.24_spmd.clone.clone, body=%wide.region_19.23_spmd.sunk.clone.clone.sunk | while | flops 675940864 | bytes 15043730 | solution.py:160
  533.1 14.0 %conditional.17 = ((f32[2560,2,128]{0,2,1:T(8,128)}, f32[2560,2,128]{0,2,1:T(8,128)}, f32[2560,2,128]{0,2,1:T(8,128)S(1)})) conditional(s32[]{:T(128)} %bitcast.135, (f32[2560,2,128]{0,2,1:T(8,128)}, f32[2560,2,128]{0,2,1:T(8,128)}, f32[2560,2,128]{0,2,1:T(8,128)S(1)}) %tuple.202, (s32[]{:T(128)}, f32[2560,2,128]{0,2,1:T(8,128)}, ...), branch_computations={%region_20.21_spmd, %region_21.22_spmd.clone} | conditional | flops 675940864 | bytes 15033202 | solution.py:157
  548.4 14.1 %conditional.17 = ((f32[2560,2,128]{0,2,1:T(8,128)}, f32[2560,2,128]{0,2,1:T(8,128)}, f32[2560,2,128]{0,2,1:T(8,128)S(1)})) conditional(s32[]{:T(128)} %bitcast.135, (f32[2560,2,128]{0,2,1:T(8,128)}, f32[2560,2,128]{0,2,1:T(8,128)}, f32[2560,2,128]{0,2,1:T(8,128)S(1)}) %tuple.202, (s32[]{:T(128)}, f32[2560,2,128]{0,2,1:T(8,128)}, ...), branch_computations={%region_20.21_spmd, %region_21.22_spmd.clone} | conditional | flops 675940864 | bytes 15033202 | solution.py:157
  563.7 14.0 %conditional.17 = ((f32[2560,2,128]{0,2,1:T(8,128)}, f32[2560,2,128]{0,2,1:T(8,128)}, f32[2560,2,128]{0,2,1:T(8,128)S(1)})) conditional(s32[]{:T(128)} %bitcast.135, (f32[2560,2,128]{0,2,1:T(8,128)}, f32[2560,2,128]{0,2,1:T(8,128)}, f32[2560,2,128]{0,2,1:T(8,128)S(1)}) %tuple.202, (s32[]{:T(128)}, f32[2560,2,128]{0,2,1:T(8,128)}, ...), branch_computations={%region_20.21_spmd, %region_21.22_spmd.clone} | conditional | flops 675940864 | bytes 15033202 | solution.py:157
  579.0 14.0 %conditional.17 = ((f32[2560,2,128]{0,2,1:T(8,128)}, f32[2560,2,128]{0,2,1:T(8,128)}, f32[2560,2,128]{0,2,1:T(8,128)S(1)})) conditional(s32[]{:T(128)} %bitcast.135, (f32[2560,2,128]{0,2,1:T(8,128)}, f32[2560,2,128]{0,2,1:T(8,128)}, f32[2560,2,128]{0,2,1:T(8,128)S(1)}) %tuple.202, (s32[]{:T(128)}, f32[2560,2,128]{0,2,1:T(8,128)}, ...), branch_computations={%region_20.21_spmd, %region_21.22_spmd.clone} | conditional | flops 675940864 | bytes 15033202 | solution.py:157
  594.3 14.0 %conditional.17 = ((f32[2560,2,128]{0,2,1:T(8,128)}, f32[2560,2,128]{0,2,1:T(8,128)}, f32[2560,2,128]{0,2,1:T(8,128)S(1)})) conditional(s32[]{:T(128)} %bitcast.135, (f32[2560,2,128]{0,2,1:T(8,128)}, f32[2560,2,128]{0,2,1:T(8,128)}, f32[2560,2,128]{0,2,1:T(8,128)S(1)}) %tuple.202, (s32[]{:T(128)}, f32[2560,2,128]{0,2,1:T(8,128)}, ...), branch_computations={%region_20.21_spmd, %region_21.22_spmd.clone} | conditional | flops 675940864 | bytes 15033202 | solution.py:157
  609.6 14.0 %conditional.17 = ((f32[2560,2,128]{0,2,1:T(8,128)}, f32[2560,2,128]{0,2,1:T(8,128)}, f32[2560,2,128]{0,2,1:T(8,128)S(1)})) conditional(s32[]{:T(128)} %bitcast.135, (f32[2560,2,128]{0,2,1:T(8,128)}, f32[2560,2,128]{0,2,1:T(8,128)}, f32[2560,2,128]{0,2,1:T(8,128)S(1)}) %tuple.202, (s32[]{:T(128)}, f32[2560,2,128]{0,2,1:T(8,128)}, ...), branch_computations={%region_20.21_spmd, %region_21.22_spmd.clone} | conditional | flops 675940864 | bytes 15033202 | solution.py:157
  624.9 14.0 %conditional.17 = ((f32[2560,2,128]{0,2,1:T(8,128)}, f32[2560,2,128]{0,2,1:T(8,128)}, f32[2560,2,128]{0,2,1:T(8,128)S(1)})) conditional(s32[]{:T(128)} %bitcast.135, (f32[2560,2,128]{0,2,1:T(8,128)}, f32[2560,2,128]{0,2,1:T(8,128)}, f32[2560,2,128]{0,2,1:T(8,128)S(1)}) %tuple.202, (s32[]{:T(128)}, f32[2560,2,128]{0,2,1:T(8,128)}, ...), branch_computations={%region_20.21_spmd, %region_21.22_spmd.clone} | conditional | flops 675940864 | bytes 15033202 | solution.py:157
  640.2 13.9 %conditional.17 = ((f32[2560,2,128]{0,2,1:T(8,128)}, f32[2560,2,128]{0,2,1:T(8,128)}, f32[2560,2,128]{0,2,1:T(8,128)S(1)})) conditional(s32[]{:T(128)} %bitcast.135, (f32[2560,2,128]{0,2,1:T(8,128)}, f32[2560,2,128]{0,2,1:T(8,128)}, f32[2560,2,128]{0,2,1:T(8,128)S(1)}) %tuple.202, (s32[]{:T(128)}, f32[2560,2,128]{0,2,1:T(8,128)}, ...), branch_computations={%region_20.21_spmd, %region_21.22_spmd.clone} | conditional | flops 675940864 | bytes 15033202 | solution.py:157
  655.4 14.0 %conditional.17 = ((f32[2560,2,128]{0,2,1:T(8,128)}, f32[2560,2,128]{0,2,1:T(8,128)}, f32[2560,2,128]{0,2,1:T(8,128)S(1)})) conditional(s32[]{:T(128)} %bitcast.135, (f32[2560,2,128]{0,2,1:T(8,128)}, f32[2560,2,128]{0,2,1:T(8,128)}, f32[2560,2,128]{0,2,1:T(8,128)S(1)}) %tuple.202, (s32[]{:T(128)}, f32[2560,2,128]{0,2,1:T(8,128)}, ...), branch_computations={%region_20.21_spmd, %region_21.22_spmd.clone} | conditional | flops 675940864 | bytes 15033202 | solution.py:157
  670.6 14.0 %conditional.17 = ((f32[2560,2,128]{0,2,1:T(8,128)}, f32[2560,2,128]{0,2,1:T(8,128)}, f32[2560,2,128]{0,2,1:T(8,128)S(1)})) conditional(s32[]{:T(128)} %bitcast.135, (f32[2560,2,128]{0,2,1:T(8,128)}, f32[2560,2,128]{0,2,1:T(8,128)}, f32[2560,2,128]{0,2,1:T(8,128)S(1)}) %tuple.202, (s32[]{:T(128)}, f32[2560,2,128]{0,2,1:T(8,128)}, ...), branch_computations={%region_20.21_spmd, %region_21.22_spmd.clone} | conditional | flops 675940864 | bytes 15033202 | solution.py:157
  686.0 14.0 %conditional.17 = ((f32[2560,2,128]{0,2,1:T(8,128)}, f32[2560,2,128]{0,2,1:T(8,128)}, f32[2560,2,128]{0,2,1:T(8,128)S(1)})) conditional(s32[]{:T(128)} %bitcast.135, (f32[2560,2,128]{0,2,1:T(8,128)}, f32[2560,2,128]{0,2,1:T(8,128)}, f32[2560,2,128]{0,2,1:T(8,128)S(1)}) %tuple.202, (s32[]{:T(128)}, f32[2560,2,128]{0,2,1:T(8,128)}, ...), branch_computations={%region_20.21_spmd, %region_21.22_spmd.clone} | conditional | flops 675940864 | bytes 15033202 | solution.py:157
  701.2 14.0 %conditional.17 = ((f32[2560,2,128]{0,2,1:T(8,128)}, f32[2560,2,128]{0,2,1:T(8,128)}, f32[2560,2,128]{0,2,1:T(8,128)S(1)})) conditional(s32[]{:T(128)} %bitcast.135, (f32[2560,2,128]{0,2,1:T(8,128)}, f32[2560,2,128]{0,2,1:T(8,128)}, f32[2560,2,128]{0,2,1:T(8,128)S(1)}) %tuple.202, (s32[]{:T(128)}, f32[2560,2,128]{0,2,1:T(8,128)}, ...), branch_computations={%region_20.21_spmd, %region_21.22_spmd.clone} | conditional | flops 675940864 | bytes 15033202 | solution.py:157
  716.5 14.0 %conditional.17 = ((f32[2560,2,128]{0,2,1:T(8,128)}, f32[2560,2,128]{0,2,1:T(8,128)}, f32[2560,2,128]{0,2,1:T(8,128)S(1)})) conditional(s32[]{:T(128)} %bitcast.135, (f32[2560,2,128]{0,2,1:T(8,128)}, f32[2560,2,128]{0,2,1:T(8,128)}, f32[2560,2,128]{0,2,1:T(8,128)S(1)}) %tuple.202, (s32[]{:T(128)}, f32[2560,2,128]{0,2,1:T(8,128)}, ...), branch_computations={%region_20.21_spmd, %region_21.22_spmd.clone} | conditional | flops 675940864 | bytes 15033202 | solution.py:157
  731.8 14.1 %conditional.17 = ((f32[2560,2,128]{0,2,1:T(8,128)}, f32[2560,2,128]{0,2,1:T(8,128)}, f32[2560,2,128]{0,2,1:T(8,128)S(1)})) conditional(s32[]{:T(128)} %bitcast.135, (f32[2560,2,128]{0,2,1:T(8,128)}, f32[2560,2,128]{0,2,1:T(8,128)}, f32[2560,2,128]{0,2,1:T(8,128)S(1)}) %tuple.202, (s32[]{:T(128)}, f32[2560,2,128]{0,2,1:T(8,128)}, ...), branch_computations={%region_20.21_spmd, %region_21.22_spmd.clone} | conditional | flops 675940864 | bytes 15033202 | solution.py:157
  747.1 14.0 %conditional.17 = ((f32[2560,2,128]{0,2,1:T(8,128)}, f32[2560,2,128]{0,2,1:T(8,128)}, f32[2560,2,128]{0,2,1:T(8,128)S(1)})) conditional(s32[]{:T(128)} %bitcast.135, (f32[2560,2,128]{0,2,1:T(8,128)}, f32[2560,2,128]{0,2,1:T(8,128)}, f32[2560,2,128]{0,2,1:T(8,128)S(1)}) %tuple.202, (s32[]{:T(128)}, f32[2560,2,128]{0,2,1:T(8,128)}, ...), branch_computations={%region_20.21_spmd, %region_21.22_spmd.clone} | conditional | flops 675940864 | bytes 15033202 | solution.py:157
  767.8 6.8 all-to-all-start.8
  781.2 10.1 all-to-all-done.8
  799.9 11.6 %all-to-all-done.10 = bf16[160,16,1,2,128]{4,0,3,2,1:T(8,128)(2,1)} async-done(((bf16[160,16,1,2,128]{4,0,3,2,1:T(8,128)(2,1)}), bf16[160,16,1,2,128]{4,0,3,2,1:T(8,128)(2,1)}, u32[]{:S(2)}, u32[]{:S(2)}) %all-to-all-start.10) | async-done | bytes 1310752 | tf_op jit(solution)/shard_map/all_to_all | solution.py:192
  817.7 13.2 %all-to-all-done.12 = bf16[160,16,1,2,128]{4,0,3,2,1:T(8,128)(2,1)S(1)} async-done(((bf16[160,16,1,2,128]{4,0,3,2,1:T(8,128)(2,1)}), bf16[160,16,1,2,128]{4,0,3,2,1:T(8,128)(2,1)S(1)}, u32[]{:S(2)}, u32[]{:S(2)}) %all-to-all-start.12) | async-done | bytes 1310752 | tf_op jit(solution)/shard_map/all_to_all | solution.py:193
  843.2 7.2 all-to-all-done.6
  850.5 12.8 %all-to-all-start.9 = ((bf16[10,16,4096]{2,0,1:T(8,128)(2,1)}), bf16[10,16,4096]{2,0,1:T(8,128)(2,1)S(1)}, u32[]{:S(2)}, u32[]{:S(2)}) async-start(bf16[10,16,4096]{2,0,1:T(8,128)(2,1)} %copy.177), calls=%async_computation.9 | async-start | bytes 4194304 | tf_op jit(solution)/shard_map/all_to_all | solution.py:199
  874.4 37.7 %all-to-all-done.9 = bf16[10,16,4096]{2,0,1:T(8,128)(2,1)S(1)} async-done(((bf16[10,16,4096]{2,0,1:T(8,128)(2,1)}), bf16[10,16,4096]{2,0,1:T(8,128)(2,1)S(1)}, u32[]{:S(2)}, u32[]{:S(2)}) %all-to-all-start.9) | async-done | bytes 1310752 | tf_op jit(solution)/shard_map/all_to_all | solution.py:199
  928.2 37.9 %all-to-all-done.11 = bf16[10,16,4096]{2,0,1:T(8,128)(2,1)} async-done(((bf16[10,16,4096]{2,0,1:T(8,128)(2,1)}), bf16[10,16,4096]{2,0,1:T(8,128)(2,1)}, u32[]{:S(2)}, u32[]{:S(2)}) %all-to-all-start.11) | async-done | bytes 1310752 | tf_op jit(solution)/shard_map/all_to_all | solution.py:200
  983.4 37.0 %all-to-all-done.13 = bf16[10,16,4096]{2,0,1:T(8,128)(2,1)} async-done(((bf16[10,16,4096]{2,0,1:T(8,128)(2,1)}), bf16[10,16,4096]{2,0,1:T(8,128)(2,1)}, u32[]{:S(2)}, u32[]{:S(2)}) %all-to-all-start.13) | async-done | bytes 1310752 | tf_op jit(solution)/shard_map/all_to_all | solution.py:201
  (800 shorter events, 570.8 us)
Async XLA Ops:
  0.6 13.5 %copy-start = (bf16[128,1,4096]{2,0,1:T(8,128)(2,1)S(1)}, bf16[128,1,4096]{2,0,1:T(8,128)(2,1)}, u32[]{:S(2)}) copy-start(bf16[128,1,4096]{2,0,1:T(8,128)(2,1)} %param.26) | copy-start | bytes 3145732
  5.9 7.7 copy-start.10
  5.9 7.7 copy-start.13
  5.9 30.5 %all-to-all-start.7 = ((bf16[160,1,16,2,128]{4,0,3,1,2:T(8,128)(2,1)}), bf16[160,1,16,2,128]{4,0,3,1,2:T(8,128)(2,1)S(1)}, u32[]{:S(2)}, u32[]{:S(2)}) async-start(bf16[160,1,16,2,128]{4,0,3,1,2:T(8,128)(2,1)} %copy.172), calls=%async_computation.7 | async-start | bytes 2621440 | tf_op jit(solution)/shard_map/all_to_all | solution.py:184
  14.2 2.4 copy-start.2
  16.6 2.4 copy-start.3
  150.7 52.1 %all-to-all-start = ((bf16[10,16,4096]{2,0,1:T(8,128)(2,1)}), bf16[10,16,4096]{2,0,1:T(8,128)(2,1)S(1)}, u32[]{:S(2)}, u32[]{:S(2)}) async-start(bf16[10,16,4096]{2,0,1:T(8,128)(2,1)} %get-tuple-element.1228), calls=%async_computation | async-start | bytes 4194304 | tf_op jit(solution)/shard_map/all_to_all | solution.py:175
  202.8 27.4 %all-to-all-start.3 = ((bf16[160,1,16,2,128]{4,0,3,1,2:T(8,128)(2,1)}), bf16[160,1,16,2,128]{4,0,3,1,2:T(8,128)(2,1)}, u32[]{:S(2)}, u32[]{:S(2)}) async-start(bf16[160,1,16,2,128]{4,0,3,1,2:T(8,128)(2,1)} %copy.162), calls=%async_computation.3 | async-start | bytes 2621440 | tf_op jit(solution)/shard_map/all_to_all | solution.py:182
  230.2 22.2 %all-to-all-start.5 = ((bf16[160,1,16,2,128]{4,0,3,1,2:T(8,128)(2,1)}), bf16[160,1,16,2,128]{4,0,3,1,2:T(8,128)(2,1)}, u32[]{:S(2)}, u32[]{:S(2)}) async-start(bf16[160,1,16,2,128]{4,0,3,1,2:T(8,128)(2,1)} %copy.166), calls=%async_computation.5 | async-start | bytes 2621440 | tf_op jit(solution)/shard_map/all_to_all | solution.py:181
  243.5 16.1 %copy-start.12 = (s32[15]{0:T(128)S(1)}, s32[15]{0:T(128)}, u32[]{:S(2)}) copy-start(s32[15]{0:T(128)} %constant.203) | copy-start | bytes 184
  252.5 135.6 %all-to-all-start.1 = ((bf16[160,1,16,2,128]{4,0,3,1,2:T(8,128)(2,1)}), bf16[160,1,16,2,128]{4,0,3,1,2:T(8,128)(2,1)}, u32[]{:S(2)}, u32[]{:S(2)}) async-start(bf16[160,1,16,2,128]{4,0,3,1,2:T(8,128)(2,1)} %copy.158), calls=%async_computation.1 | async-start | bytes 2621440 | tf_op jit(solution)/shard_map/all_to_all | solution.py:183
  257.6 3.5 copy-start.11
  263.5 263.0 %copy-start.4 = (bf16[160,1,16,2,128]{4,2,0,3,1:T(8,128)(2,1)}, bf16[160,1,16,2,128]{4,2,0,3,1:T(8,128)(2,1)S(1)}, u32[]{:S(2)}) copy-start(bf16[160,1,16,2,128]{4,2,0,3,1:T(8,128)(2,1)S(1)} %copy.173) | copy-start | bytes 3932164
  387.0 1.1 copy-start.8
  390.2 3.5 copy-start.5
  526.5 1.1 copy-start.6
  767.8 23.5 %all-to-all-start.8 = ((bf16[160,16,1,2,128]{4,0,3,2,1:T(8,128)(2,1)}), bf16[160,16,1,2,128]{4,0,3,2,1:T(8,128)(2,1)}, u32[]{:S(2)}, u32[]{:S(2)}) async-start(bf16[160,16,1,2,128]{4,0,3,2,1:T(8,128)(2,1)} %copy.175), calls=%async_computation.8 | async-start | bytes 2621440 | tf_op jit(solution)/shard_map/all_to_all | solution.py:191
  791.3 20.2 %all-to-all-start.10 = ((bf16[160,16,1,2,128]{4,0,3,2,1:T(8,128)(2,1)}), bf16[160,16,1,2,128]{4,0,3,2,1:T(8,128)(2,1)}, u32[]{:S(2)}, u32[]{:S(2)}) async-start(bf16[160,16,1,2,128]{4,0,3,2,1:T(8,128)(2,1)} %copy.180), calls=%async_computation.10 | async-start | bytes 2621440 | tf_op jit(solution)/shard_map/all_to_all | solution.py:192
  799.9 15.3 %copy-start.7 = (bf16[2560,2,128]{2,0,1:T(8,128)(2,1)S(1)}, bf16[2560,2,128]{2,0,1:T(8,128)(2,1)}, u32[]{:S(2)}) copy-start(bf16[2560,2,128]{2,0,1:T(8,128)(2,1)} %copy-done.6) | copy-start | bytes 3932164
  811.5 19.3 %all-to-all-start.12 = ((bf16[160,16,1,2,128]{4,0,3,2,1:T(8,128)(2,1)}), bf16[160,16,1,2,128]{4,0,3,2,1:T(8,128)(2,1)S(1)}, u32[]{:S(2)}, u32[]{:S(2)}) async-start(bf16[160,16,1,2,128]{4,0,3,2,1:T(8,128)(2,1)} %copy.185), calls=%async_computation.12 | async-start | bytes 2621440 | tf_op jit(solution)/shard_map/all_to_all | solution.py:193
  830.8 1.1 copy-start.9
  831.9 18.6 %all-to-all-start.6 = ((bf16[160,16,1,2,128]{4,3,0,2,1:T(2,128)(2,1)}), bf16[160,16,1,2,128]{4,3,0,2,1:T(2,128)(2,1)S(1)}, u32[]{:S(2)}, u32[]{:S(2)}) async-start(bf16[160,16,1,2,128]{4,3,0,2,1:T(2,128)(2,1)} %copy.170), calls=%async_computation.6 | async-start | bytes 2621440 | tf_op jit(solution)/shard_map/all_to_all | solution.py:190
  850.5 61.7 %all-to-all-start.9 = ((bf16[10,16,4096]{2,0,1:T(8,128)(2,1)}), bf16[10,16,4096]{2,0,1:T(8,128)(2,1)S(1)}, u32[]{:S(2)}, u32[]{:S(2)}) async-start(bf16[10,16,4096]{2,0,1:T(8,128)(2,1)} %copy.177), calls=%async_computation.9 | async-start | bytes 4194304 | tf_op jit(solution)/shard_map/all_to_all | solution.py:199
  912.1 54.0 %all-to-all-start.11 = ((bf16[10,16,4096]{2,0,1:T(8,128)(2,1)}), bf16[10,16,4096]{2,0,1:T(8,128)(2,1)}, u32[]{:S(2)}, u32[]{:S(2)}) async-start(bf16[10,16,4096]{2,0,1:T(8,128)(2,1)} %copy.182), calls=%async_computation.11 | async-start | bytes 4194304 | tf_op jit(solution)/shard_map/all_to_all | solution.py:200
  966.2 54.2 %all-to-all-start.13 = ((bf16[10,16,4096]{2,0,1:T(8,128)(2,1)}), bf16[10,16,4096]{2,0,1:T(8,128)(2,1)}, u32[]{:S(2)}, u32[]{:S(2)}) async-start(bf16[10,16,4096]{2,0,1:T(8,128)(2,1)} %copy.187), calls=%async_computation.13 | async-start | bytes 4194304 | tf_op jit(solution)/shard_map/all_to_all | solution.py:201
  1024.9 3.1 copy-start.1
where the time goes:
time: 1040 us; the launch traced here: 1030 us
  local copies, waits for them, and re-layouts  283 us (27%)
  waiting for transfers between devices  211 us (20%)
  matrix products  210 us (20%)
  blocking collectives  114 us (11%)
  loops' own time  92.3 us (9%)
  starting transfers between devices  69.7 us (7%)
  other arithmetic  46.9 us (5%)
    all_to_all x1, blocking collectives, to_groups(): lax.all_to_all(second_part, 'dp', split_axis=1, concat_axis=1, tiled=True)  60.6 us
    dynamic_slice x45, local copies, waits for them, and re-layouts, tile_scores(): q_start = query_block[pair_index] * block_rows  56.3 us
    dynamic_slice x45, local copies, waits for them, and re-layouts, tile_scores(): k_start = key_block[pair_index] * block_rows  56.3 us
    all_to_all x1, blocking collectives, to_groups(): lax.all_to_all(first_part, 'dp', split_axis=1, concat_axis=1, tiled=True)  53.7 us
    dot_general x30, matrix products, tile_scores(): jnp.einsum('qhe,khe->qhk', q_rows, k_rows, preferred_element_type=jnp.flo...  49.3 us
    dot_general x15, matrix products, value_compute(): jnp.einsum('qhk,khe->qhe', weight, v_rows, preferred_element_type=jnp.flo...  44.9 us
    all_to_all x1, waiting for transfers between devices, to_packed(): lax.all_to_all(second_part, 'dp', split_axis=1, concat_axis=1, tiled=True)  37.9 us
    all_to_all x1, waiting for transfers between devices, to_packed(): lax.all_to_all(first_part, 'dp', split_axis=1, concat_axis=1, tiled=True)  37.7 us
  transfers between devices with their start and end apart: 12, of which 10 were waited for; matrix products, arithmetic and copies ran while one was open for 20% of the time, Pallas kernels for 0%

commit v1 on v0

--- a/solution.py
+++ b/solution.py
@@ -6,6 +6,9 @@
 
 HEAD = 128
 NEGATIVE_FILL = -1e30
+fit_floor = lambda x_local: jnp.concatenate(
+    lax.all_to_all(jnp.stack(jnp.split(x_local, lax.axis_size("dp"), axis=1)), "dp", 0, 0), axis=1
+)
 
 
 def group_tables(doc_lengths, doc_group, group_count, per_unit):
@@ -198,7 +201,7 @@
     return (
         lax.all_to_all(first_part, "dp", split_axis=1, concat_axis=1, tiled=True),
         lax.all_to_all(second_part, "dp", split_axis=1, concat_axis=1, tiled=True),
-        lax.all_to_all(third_part, "dp", split_axis=1, concat_axis=1, tiled=True),
+        fit_floor(third_part),
     )
 
 

time: 1040 us -> 1040 us (level)
    unnamed x29 -> x54, local copies, waits for them, and re-layouts: 4.04 us -> 14.8 us
    all_to_all x1, waiting for transfers between devices: 13.2 us -> 2.43 us  [from_heads(): lax.all_to_all(fourth_part, 'seq', split_axis=1, concat_axis=2, tiled=True)]
  transfers between devices with their start and end apart: 12 -> 12, of which waited for: 10 -> 9; matrix products, arithmetic and copies ran while one was open for 20% -> 20% of each run, Pallas kernels for 0% -> 0%
where the time goes in v1:
time: 1040 us; the launch traced here: 1030 us
  local copies, waits for them, and re-layouts  283 us (27%)
  matrix products  211 us (20%)
  waiting for transfers between devices  210 us (20%)
  blocking collectives  114 us (11%)
  loops' own time  88.7 us (9%)
  starting transfers between devices  72.4 us (7%)
  other arithmetic  46.9 us (5%)
    all_to_all x1, blocking collectives, to_groups(): lax.all_to_all(second_part, 'dp', split_axis=1, concat_axis=1, tiled=True)  60.6 us
    dynamic_slice x45, local copies, waits for them, and re-layouts, tile_scores(): q_start = query_block[pair_index] * block_rows  55.9 us
    dynamic_slice x45, local copies, waits for them, and re-layouts, tile_scores(): k_start = key_block[pair_index] * block_rows  55.9 us
    all_to_all x1, blocking collectives, to_groups(): lax.all_to_all(first_part, 'dp', split_axis=1, concat_axis=1, tiled=True)  53.7 us
    dot_general x30, matrix products, tile_scores(): jnp.einsum('qhe,khe->qhk', q_rows, k_rows, preferred_element_type=jnp.flo...  49.3 us
    dot_general x15, matrix products, value_compute(): jnp.einsum('qhk,khe->qhe', weight, v_rows, preferred_element_type=jnp.flo...  45.1 us
    all_to_all x1, waiting for transfers between devices, lax.all_to_all(jnp.stack(jnp.split(x_local, lax.axis_size('dp'), axis=1))...  41.4 us
    all_to_all x1, waiting for transfers between devices, to_packed(): lax.all_to_all(first_part, 'dp', split_axis=1, concat_axis=1, tiled=True)  41.3 us
  transfers between devices with their start and end apart: 12, of which 9 were waited for; matrix products, arithmetic and copies ran while one was open for 20% of the time, Pallas kernels for 0%

profile of v1, /device:TPU:1, one launch (start us, length us, event | category | flops | bytes accessed | tf_op | source)
XLA Modules:
  0.0 1027.9 jit_solution(17507517473948000731)
XLA Ops:
  5.9 7.6 all-to-all-start.7
  25.8 10.6 %copy_select_fusion = (bf16[10,16,4096]{2,0,1:T(8,128)(2,1)S(1)}, bf16[10,16,4096]{2,0,1:T(8,128)(2,1)}, bf16[10,16,4096]{2,0,1:T(8,128)(2,1)}) fusion(bf16[10,16,4096]{2,1,0:T(8,128)(2,1)} %bitcast.186, pred[10,16]{0,1:T(8,128)(4,1)S(1)} %copy.597, bf16[10,16,4096]{2,1,0:T(8,128)(2,1)} %bitcast.187, bf16[10,16,4096]{2,1,0:T(8,128)(2,1)} %bitcast.188), kind=kLoop, calls=%fused_computation.84 | loop fusion | flops 1966080 | bytes 7864480 | tf_op jit(solution)/shard_map/jit(_where)/select_n | solution.py:238
  36.3 60.6 %all_to_all.102 = bf16[10,16,4096]{2,0,1:T(8,128)(2,1)} all-to-all(bf16[10,16,4096]{2,0,1:T(8,128)(2,1)} %get-tuple-element.1383), channel_id=1, replica_groups=mesh['seq'=16,'dp'=16] {'dp'}, dimensions={1} | all-to-all | bytes 2621440 | tf_op jit(solution)/shard_map/all_to_all | solution.py:177
  96.9 53.7 %all_to_all.103 = bf16[10,16,4096]{2,0,1:T(8,128)(2,1)} all-to-all(bf16[10,16,4096]{2,0,1:T(8,128)(2,1)S(1)} %get-tuple-element.1382), channel_id=1, replica_groups=mesh['seq'=16,'dp'=16] {'dp'}, dimensions={1} | all-to-all | bytes 2621440 | tf_op jit(solution)/shard_map/all_to_all | solution.py:176
  165.1 37.7 %all-to-all-done = bf16[10,16,4096]{2,0,1:T(8,128)(2,1)S(1)} async-done(((bf16[10,16,4096]{2,0,1:T(8,128)(2,1)}), bf16[10,16,4096]{2,0,1:T(8,128)(2,1)S(1)}, u32[]{:S(2)}, u32[]{:S(2)}) %all-to-all-start) | async-done | bytes 1310752 | tf_op jit(solution)/shard_map/all_to_all | solution.py:178
  202.8 7.0 all-to-all-start.3
  220.4 9.8 all-to-all-done.3
  242.8 9.7 all-to-all-done.5
  270.2 113.0 %while.54 = (s32[]{:T(128)}, f32[2560,2]{0,1:T(2,128)S(1)}, f32[2560,2]{0,1:T(2,128)S(1)}, pred[15]{0:T(512)(128)(4,1)S(1)}, s32[2560]{0:T(1024)S(1)}, /*index=5...) while((s32[]{:T(128)}, f32[2560,2]{0,1:T(2,128)S(1)}, ...), condition=%wide.region_13.15_spmd.clone.clone, body=%wide.region_8.14_spmd.sunk.clone.clone.sunk | while | flops 138678800 | bytes 5712918 | solution.py:88
  271.4 6.3 conditional.15
  278.9 6.3 conditional.15
  286.4 6.3 conditional.15
  294.0 6.3 conditional.15
  301.5 6.3 conditional.15
  309.0 6.3 conditional.15
  316.6 6.3 conditional.15
  324.1 6.3 conditional.15
  331.6 6.3 conditional.15
  339.2 6.3 conditional.15
  346.7 6.3 conditional.15
  354.2 6.3 conditional.15
  361.8 6.3 conditional.15
  369.3 6.3 conditional.15
  376.8 6.3 conditional.15
  389.9 131.0 %while.55 = (s32[]{:T(128)}, f32[2560,2,128]{0,2,1:T(8,128)}, pred[15]{0:T(512)(128)(4,1)S(1)}, bf16[2560,2,128]{0,2,1:T(8,128)(2,1)}, s32[2560]{0:T(1024)S(1)},...) while((s32[]{:T(128)}, f32[2560,2,128]{0,2,1:T(8,128)}, ...), condition=%wide.region_17.19_spmd.clone.clone, body=%wide.region_14.18_spmd.sunk.clone.clone.sunk | while | flops 271452672 | bytes 2450426 | solution.py:108
  391.1 7.5 conditional.16
  399.9 7.4 conditional.16
  408.6 7.4 conditional.16
  417.3 7.5 conditional.16
  426.0 7.5 conditional.16
  434.7 7.5 conditional.16
  443.4 7.5 conditional.16
  452.1 7.5 conditional.16
  460.9 7.5 conditional.16
  469.6 7.5 conditional.16
  478.3 7.5 conditional.16
  487.1 7.5 conditional.16
  495.8 7.5 conditional.16
  504.6 7.5 conditional.16
  513.4 7.5 conditional.16
  527.7 229.7 %while.56 = (s32[]{:T(128)}, f32[2560,2,128]{0,2,1:T(8,128)}, f32[2560,2,128]{0,2,1:T(8,128)}, f32[2560,2,128]{0,2,1:T(8,128)S(1)}, pred[15]{0:T(512)(128)(4,1)S...) while((s32[]{:T(128)}, f32[2560,2,128]{0,2,1:T(8,128)}, ...), condition=%wide.region_22.24_spmd.clone.clone, body=%wide.region_19.23_spmd.sunk.clone.clone.sunk | while | flops 675940864 | bytes 15043730 | solution.py:163
  529.2 14.0 %conditional.17 = ((f32[2560,2,128]{0,2,1:T(8,128)}, f32[2560,2,128]{0,2,1:T(8,128)}, f32[2560,2,128]{0,2,1:T(8,128)S(1)})) conditional(s32[]{:T(128)} %bitcast.168, (f32[2560,2,128]{0,2,1:T(8,128)}, f32[2560,2,128]{0,2,1:T(8,128)}, f32[2560,2,128]{0,2,1:T(8,128)S(1)}) %tuple.232, (s32[]{:T(128)}, f32[2560,2,128]{0,2,1:T(8,128)}, ...), branch_computations={%region_20.21_spmd, %region_21.22_spmd.clone} | conditional | flops 675940864 | bytes 15033202 | solution.py:160
  544.5 14.0 %conditional.17 = ((f32[2560,2,128]{0,2,1:T(8,128)}, f32[2560,2,128]{0,2,1:T(8,128)}, f32[2560,2,128]{0,2,1:T(8,128)S(1)})) conditional(s32[]{:T(128)} %bitcast.168, (f32[2560,2,128]{0,2,1:T(8,128)}, f32[2560,2,128]{0,2,1:T(8,128)}, f32[2560,2,128]{0,2,1:T(8,128)S(1)}) %tuple.232, (s32[]{:T(128)}, f32[2560,2,128]{0,2,1:T(8,128)}, ...), branch_computations={%region_20.21_spmd, %region_21.22_spmd.clone} | conditional | flops 675940864 | bytes 15033202 | solution.py:160
  559.7 14.0 %conditional.17 = ((f32[2560,2,128]{0,2,1:T(8,128)}, f32[2560,2,128]{0,2,1:T(8,128)}, f32[2560,2,128]{0,2,1:T(8,128)S(1)})) conditional(s32[]{:T(128)} %bitcast.168, (f32[2560,2,128]{0,2,1:T(8,128)}, f32[2560,2,128]{0,2,1:T(8,128)}, f32[2560,2,128]{0,2,1:T(8,128)S(1)}) %tuple.232, (s32[]{:T(128)}, f32[2560,2,128]{0,2,1:T(8,128)}, ...), branch_computations={%region_20.21_spmd, %region_21.22_spmd.clone} | conditional | flops 675940864 | bytes 15033202 | solution.py:160
  575.0 14.0 %conditional.17 = ((f32[2560,2,128]{0,2,1:T(8,128)}, f32[2560,2,128]{0,2,1:T(8,128)}, f32[2560,2,128]{0,2,1:T(8,128)S(1)})) conditional(s32[]{:T(128)} %bitcast.168, (f32[2560,2,128]{0,2,1:T(8,128)}, f32[2560,2,128]{0,2,1:T(8,128)}, f32[2560,2,128]{0,2,1:T(8,128)S(1)}) %tuple.232, (s32[]{:T(128)}, f32[2560,2,128]{0,2,1:T(8,128)}, ...), branch_computations={%region_20.21_spmd, %region_21.22_spmd.clone} | conditional | flops 675940864 | bytes 15033202 | solution.py:160
  590.3 14.1 %conditional.17 = ((f32[2560,2,128]{0,2,1:T(8,128)}, f32[2560,2,128]{0,2,1:T(8,128)}, f32[2560,2,128]{0,2,1:T(8,128)S(1)})) conditional(s32[]{:T(128)} %bitcast.168, (f32[2560,2,128]{0,2,1:T(8,128)}, f32[2560,2,128]{0,2,1:T(8,128)}, f32[2560,2,128]{0,2,1:T(8,128)S(1)}) %tuple.232, (s32[]{:T(128)}, f32[2560,2,128]{0,2,1:T(8,128)}, ...), branch_computations={%region_20.21_spmd, %region_21.22_spmd.clone} | conditional | flops 675940864 | bytes 15033202 | solution.py:160
  605.6 14.0 %conditional.17 = ((f32[2560,2,128]{0,2,1:T(8,128)}, f32[2560,2,128]{0,2,1:T(8,128)}, f32[2560,2,128]{0,2,1:T(8,128)S(1)})) conditional(s32[]{:T(128)} %bitcast.168, (f32[2560,2,128]{0,2,1:T(8,128)}, f32[2560,2,128]{0,2,1:T(8,128)}, f32[2560,2,128]{0,2,1:T(8,128)S(1)}) %tuple.232, (s32[]{:T(128)}, f32[2560,2,128]{0,2,1:T(8,128)}, ...), branch_computations={%region_20.21_spmd, %region_21.22_spmd.clone} | conditional | flops 675940864 | bytes 15033202 | solution.py:160
  620.9 14.0 %conditional.17 = ((f32[2560,2,128]{0,2,1:T(8,128)}, f32[2560,2,128]{0,2,1:T(8,128)}, f32[2560,2,128]{0,2,1:T(8,128)S(1)})) conditional(s32[]{:T(128)} %bitcast.168, (f32[2560,2,128]{0,2,1:T(8,128)}, f32[2560,2,128]{0,2,1:T(8,128)}, f32[2560,2,128]{0,2,1:T(8,128)S(1)}) %tuple.232, (s32[]{:T(128)}, f32[2560,2,128]{0,2,1:T(8,128)}, ...), branch_computations={%region_20.21_spmd, %region_21.22_spmd.clone} | conditional | flops 675940864 | bytes 15033202 | solution.py:160
  636.2 14.0 %conditional.17 = ((f32[2560,2,128]{0,2,1:T(8,128)}, f32[2560,2,128]{0,2,1:T(8,128)}, f32[2560,2,128]{0,2,1:T(8,128)S(1)})) conditional(s32[]{:T(128)} %bitcast.168, (f32[2560,2,128]{0,2,1:T(8,128)}, f32[2560,2,128]{0,2,1:T(8,128)}, f32[2560,2,128]{0,2,1:T(8,128)S(1)}) %tuple.232, (s32[]{:T(128)}, f32[2560,2,128]{0,2,1:T(8,128)}, ...), branch_computations={%region_20.21_spmd, %region_21.22_spmd.clone} | conditional | flops 675940864 | bytes 15033202 | solution.py:160
  651.5 14.0 %conditional.17 = ((f32[2560,2,128]{0,2,1:T(8,128)}, f32[2560,2,128]{0,2,1:T(8,128)}, f32[2560,2,128]{0,2,1:T(8,128)S(1)})) conditional(s32[]{:T(128)} %bitcast.168, (f32[2560,2,128]{0,2,1:T(8,128)}, f32[2560,2,128]{0,2,1:T(8,128)}, f32[2560,2,128]{0,2,1:T(8,128)S(1)}) %tuple.232, (s32[]{:T(128)}, f32[2560,2,128]{0,2,1:T(8,128)}, ...), branch_computations={%region_20.21_spmd, %region_21.22_spmd.clone} | conditional | flops 675940864 | bytes 15033202 | solution.py:160
  666.8 14.0 %conditional.17 = ((f32[2560,2,128]{0,2,1:T(8,128)}, f32[2560,2,128]{0,2,1:T(8,128)}, f32[2560,2,128]{0,2,1:T(8,128)S(1)})) conditional(s32[]{:T(128)} %bitcast.168, (f32[2560,2,128]{0,2,1:T(8,128)}, f32[2560,2,128]{0,2,1:T(8,128)}, f32[2560,2,128]{0,2,1:T(8,128)S(1)}) %tuple.232, (s32[]{:T(128)}, f32[2560,2,128]{0,2,1:T(8,128)}, ...), branch_computations={%region_20.21_spmd, %region_21.22_spmd.clone} | conditional | flops 675940864 | bytes 15033202 | solution.py:160
  682.0 14.0 %conditional.17 = ((f32[2560,2,128]{0,2,1:T(8,128)}, f32[2560,2,128]{0,2,1:T(8,128)}, f32[2560,2,128]{0,2,1:T(8,128)S(1)})) conditional(s32[]{:T(128)} %bitcast.168, (f32[2560,2,128]{0,2,1:T(8,128)}, f32[2560,2,128]{0,2,1:T(8,128)}, f32[2560,2,128]{0,2,1:T(8,128)S(1)}) %tuple.232, (s32[]{:T(128)}, f32[2560,2,128]{0,2,1:T(8,128)}, ...), branch_computations={%region_20.21_spmd, %region_21.22_spmd.clone} | conditional | flops 675940864 | bytes 15033202 | solution.py:160
  697.4 14.1 %conditional.17 = ((f32[2560,2,128]{0,2,1:T(8,128)}, f32[2560,2,128]{0,2,1:T(8,128)}, f32[2560,2,128]{0,2,1:T(8,128)S(1)})) conditional(s32[]{:T(128)} %bitcast.168, (f32[2560,2,128]{0,2,1:T(8,128)}, f32[2560,2,128]{0,2,1:T(8,128)}, f32[2560,2,128]{0,2,1:T(8,128)S(1)}) %tuple.232, (s32[]{:T(128)}, f32[2560,2,128]{0,2,1:T(8,128)}, ...), branch_computations={%region_20.21_spmd, %region_21.22_spmd.clone} | conditional | flops 675940864 | bytes 15033202 | solution.py:160
  712.7 14.1 %conditional.17 = ((f32[2560,2,128]{0,2,1:T(8,128)}, f32[2560,2,128]{0,2,1:T(8,128)}, f32[2560,2,128]{0,2,1:T(8,128)S(1)})) conditional(s32[]{:T(128)} %bitcast.168, (f32[2560,2,128]{0,2,1:T(8,128)}, f32[2560,2,128]{0,2,1:T(8,128)}, f32[2560,2,128]{0,2,1:T(8,128)S(1)}) %tuple.232, (s32[]{:T(128)}, f32[2560,2,128]{0,2,1:T(8,128)}, ...), branch_computations={%region_20.21_spmd, %region_21.22_spmd.clone} | conditional | flops 675940864 | bytes 15033202 | solution.py:160
  728.1 14.0 %conditional.17 = ((f32[2560,2,128]{0,2,1:T(8,128)}, f32[2560,2,128]{0,2,1:T(8,128)}, f32[2560,2,128]{0,2,1:T(8,128)S(1)})) conditional(s32[]{:T(128)} %bitcast.168, (f32[2560,2,128]{0,2,1:T(8,128)}, f32[2560,2,128]{0,2,1:T(8,128)}, f32[2560,2,128]{0,2,1:T(8,128)S(1)}) %tuple.232, (s32[]{:T(128)}, f32[2560,2,128]{0,2,1:T(8,128)}, ...), branch_computations={%region_20.21_spmd, %region_21.22_spmd.clone} | conditional | flops 675940864 | bytes 15033202 | solution.py:160
  743.4 14.0 %conditional.17 = ((f32[2560,2,128]{0,2,1:T(8,128)}, f32[2560,2,128]{0,2,1:T(8,128)}, f32[2560,2,128]{0,2,1:T(8,128)S(1)})) conditional(s32[]{:T(128)} %bitcast.168, (f32[2560,2,128]{0,2,1:T(8,128)}, f32[2560,2,128]{0,2,1:T(8,128)}, f32[2560,2,128]{0,2,1:T(8,128)S(1)}) %tuple.232, (s32[]{:T(128)}, f32[2560,2,128]{0,2,1:T(8,128)}, ...), branch_computations={%region_20.21_spmd, %region_21.22_spmd.clone} | conditional | flops 675940864 | bytes 15033202 | solution.py:160
  761.9 6.8 all-to-all-start.12
  808.4 6.8 all-to-all-start.10
  816.6 14.3 %all-to-all-done.10 = bf16[160,16,1,2,128]{4,0,3,2,1:T(8,128)(2,1)S(1)} async-done(((bf16[160,16,1,2,128]{4,0,3,2,1:T(8,128)(2,1)}), bf16[160,16,1,2,128]{4,0,3,2,1:T(8,128)(2,1)S(1)}, u32[]{:S(2)}, u32[]{:S(2)}) %all-to-all-start.10) | async-done | bytes 1310752 | tf_op jit(solution)/shard_map/all_to_all | solution.py:195
  836.8 14.1 %all-to-all-done.6 = bf16[160,16,1,2,128]{4,3,0,2,1:T(2,128)(2,1)} async-done(((bf16[160,16,1,2,128]{4,3,0,2,1:T(2,128)(2,1)}), bf16[160,16,1,2,128]{4,3,0,2,1:T(2,128)(2,1)}, u32[]{:S(2)}, u32[]{:S(2)}) %all-to-all-start.6) | async-done | bytes 1310752 | tf_op jit(solution)/shard_map/all_to_all | solution.py:193
  851.0 11.6 %all-to-all-start.13 = ((bf16[16,10,1,4096]{3,1,2,0:T(8,128)(2,1)}), bf16[16,10,1,4096]{3,1,2,0:T(8,128)(2,1)S(1)}, u32[]{:S(2)}, u32[]{:S(2)}) async-start(bf16[16,10,1,4096]{3,1,2,0:T(8,128)(2,1)} %bitcast_dynamic-update-slice_fusion), calls=%async_computation.13 | async-start | bytes 4194304 | tf_op jit(solution)/shard_map/all_to_all | solution.py:10
  870.2 41.4 %all-to-all-done.13 = bf16[16,10,1,4096]{3,1,2,0:T(8,128)(2,1)S(1)} async-done(((bf16[16,10,1,4096]{3,1,2,0:T(8,128)(2,1)}), bf16[16,10,1,4096]{3,1,2,0:T(8,128)(2,1)S(1)}, u32[]{:S(2)}, u32[]{:S(2)}) %all-to-all-start.13) | async-done | bytes 1310752 | tf_op jit(solution)/shard_map/all_to_all | solution.py:10
  924.5 41.3 %all-to-all-done.9 = bf16[10,16,4096]{2,0,1:T(8,128)(2,1)} async-done(((bf16[10,16,4096]{2,0,1:T(8,128)(2,1)}), bf16[10,16,4096]{2,0,1:T(8,128)(2,1)}, u32[]{:S(2)}, u32[]{:S(2)}) %all-to-all-start.9) | async-done | bytes 1310752 | tf_op jit(solution)/shard_map/all_to_all | solution.py:202
  980.5 39.4 %all-to-all-done.11 = bf16[10,16,4096]{2,0,1:T(8,128)(2,1)} async-done(((bf16[10,16,4096]{2,0,1:T(8,128)(2,1)}), bf16[10,16,4096]{2,0,1:T(8,128)(2,1)}, u32[]{:S(2)}, u32[]{:S(2)}) %all-to-all-start.11) | async-done | bytes 1310752 | tf_op jit(solution)/shard_map/all_to_all | solution.py:203
  (825 shorter events, 565.4 us)
Async XLA Ops:
  0.6 13.4 %copy-start = (bf16[128,1,4096]{2,0,1:T(8,128)(2,1)S(1)}, bf16[128,1,4096]{2,0,1:T(8,128)(2,1)}, u32[]{:S(2)}) copy-start(bf16[128,1,4096]{2,0,1:T(8,128)(2,1)} %param.26) | copy-start | bytes 3145732
  4.3 9.2 copy-start.15
  4.3 9.2 copy-start.18
  4.3 9.7 copy-start.17
  5.9 30.4 %all-to-all-start.7 = ((bf16[160,1,16,2,128]{4,0,3,1,2:T(8,128)(2,1)}), bf16[160,1,16,2,128]{4,0,3,1,2:T(8,128)(2,1)S(1)}, u32[]{:S(2)}, u32[]{:S(2)}) async-start(bf16[160,1,16,2,128]{4,0,3,1,2:T(8,128)(2,1)} %copy.614), calls=%async_computation.7 | async-start | bytes 2621440 | tf_op jit(solution)/shard_map/all_to_all | solution.py:187
  14.1 2.5 copy-start.2
  16.5 2.5 copy-start.3
  150.6 52.1 %all-to-all-start = ((bf16[10,16,4096]{2,0,1:T(8,128)(2,1)}), bf16[10,16,4096]{2,0,1:T(8,128)(2,1)S(1)}, u32[]{:S(2)}, u32[]{:S(2)}) async-start(bf16[10,16,4096]{2,0,1:T(8,128)(2,1)} %get-tuple-element.1384), calls=%async_computation | async-start | bytes 4194304 | tf_op jit(solution)/shard_map/all_to_all | solution.py:178
  202.8 27.4 %all-to-all-start.3 = ((bf16[160,1,16,2,128]{4,0,3,1,2:T(8,128)(2,1)}), bf16[160,1,16,2,128]{4,0,3,1,2:T(8,128)(2,1)}, u32[]{:S(2)}, u32[]{:S(2)}) async-start(bf16[160,1,16,2,128]{4,0,3,1,2:T(8,128)(2,1)} %copy.604), calls=%async_computation.3 | async-start | bytes 2621440 | tf_op jit(solution)/shard_map/all_to_all | solution.py:185
  230.2 22.3 %all-to-all-start.5 = ((bf16[160,1,16,2,128]{4,0,3,1,2:T(8,128)(2,1)}), bf16[160,1,16,2,128]{4,0,3,1,2:T(8,128)(2,1)}, u32[]{:S(2)}, u32[]{:S(2)}) async-start(bf16[160,1,16,2,128]{4,0,3,1,2:T(8,128)(2,1)} %copy.608), calls=%async_computation.5 | async-start | bytes 2621440 | tf_op jit(solution)/shard_map/all_to_all | solution.py:184
  242.8 19.1 %copy-start.16 = (s32[15]{0:T(128)S(1)}, s32[15]{0:T(128)}, u32[]{:S(2)}) copy-start(s32[15]{0:T(128)} %constant.203) | copy-start | bytes 184
  252.5 131.8 %all-to-all-start.1 = ((bf16[160,1,16,2,128]{4,0,3,1,2:T(8,128)(2,1)}), bf16[160,1,16,2,128]{4,0,3,1,2:T(8,128)(2,1)}, u32[]{:S(2)}, u32[]{:S(2)}) async-start(bf16[160,1,16,2,128]{4,0,3,1,2:T(8,128)(2,1)} %copy.600), calls=%async_computation.1 | async-start | bytes 2621440 | tf_op jit(solution)/shard_map/all_to_all | solution.py:186
  264.3 258.7 %copy-start.6 = (bf16[160,1,16,2,128]{4,2,0,3,1:T(8,128)(2,1)}, bf16[160,1,16,2,128]{4,2,0,3,1:T(8,128)(2,1)S(1)}, u32[]{:S(2)}) copy-start(bf16[160,1,16,2,128]{4,2,0,3,1:T(8,128)(2,1)S(1)} %copy.615) | copy-start | bytes 3932164
  383.2 1.1 copy-start.10
  386.4 3.5 copy-start.7
  522.9 2.6 copy-start.8
  759.0 9.8 copy-start.4
  761.9 23.5 %all-to-all-start.12 = ((bf16[160,16,1,2,128]{4,0,3,2,1:T(8,128)(2,1)}), bf16[160,16,1,2,128]{4,0,3,2,1:T(8,128)(2,1)}, u32[]{:S(2)}, u32[]{:S(2)}) async-start(bf16[160,16,1,2,128]{4,0,3,2,1:T(8,128)(2,1)} %copy.627), calls=%async_computation.12 | async-start | bytes 2621440 | tf_op jit(solution)/shard_map/all_to_all | solution.py:196
  772.9 2.2 copy-start.5
  779.2 1.4 copy-start.9
  785.5 22.9 %all-to-all-start.8 = ((bf16[160,16,1,2,128]{4,0,3,2,1:T(8,128)(2,1)}), bf16[160,16,1,2,128]{4,0,3,2,1:T(8,128)(2,1)S(1)}, u32[]{:S(2)}, u32[]{:S(2)}) async-start(bf16[160,16,1,2,128]{4,0,3,2,1:T(8,128)(2,1)} %copy.617), calls=%async_computation.8 | async-start | bytes 2621440 | tf_op jit(solution)/shard_map/all_to_all | solution.py:194
  808.4 22.6 %copy-start.11 = (bf16[160,16,1,2,128]{4,0,3,2,1:T(8,128)(2,1)}, bf16[160,16,1,2,128]{4,0,3,2,1:T(8,128)(2,1)S(1)}, u32[]{:S(2)}) copy-start(bf16[160,16,1,2,128]{4,0,3,2,1:T(8,128)(2,1)S(1)} %all-to-all-done.8) | copy-start | bytes 3932164
  808.4 22.6 %all-to-all-start.10 = ((bf16[160,16,1,2,128]{4,0,3,2,1:T(8,128)(2,1)}), bf16[160,16,1,2,128]{4,0,3,2,1:T(8,128)(2,1)S(1)}, u32[]{:S(2)}, u32[]{:S(2)}) async-start(bf16[160,16,1,2,128]{4,0,3,2,1:T(8,128)(2,1)} %copy.622), calls=%async_computation.10 | async-start | bytes 2621440 | tf_op jit(solution)/shard_map/all_to_all | solution.py:195
  830.9 5.2 copy-start.13
  830.9 20.0 %all-to-all-start.6 = ((bf16[160,16,1,2,128]{4,3,0,2,1:T(2,128)(2,1)}), bf16[160,16,1,2,128]{4,3,0,2,1:T(2,128)(2,1)}, u32[]{:S(2)}, u32[]{:S(2)}) async-start(bf16[160,16,1,2,128]{4,3,0,2,1:T(2,128)(2,1)} %copy.612), calls=%async_computation.6 | async-start | bytes 2621440 | tf_op jit(solution)/shard_map/all_to_all | solution.py:193
  836.8 25.8 %copy-start.12 = (bf16[160,16,1,2,128]{4,0,3,2,1:T(8,128)(2,1)S(1)}, bf16[160,16,1,2,128]{4,0,3,2,1:T(8,128)(2,1)}, u32[]{:S(2)}) copy-start(bf16[160,16,1,2,128]{4,0,3,2,1:T(8,128)(2,1)} %copy-done.11) | copy-start | bytes 3932164
  851.0 60.6 %all-to-all-start.13 = ((bf16[16,10,1,4096]{3,1,2,0:T(8,128)(2,1)}), bf16[16,10,1,4096]{3,1,2,0:T(8,128)(2,1)S(1)}, u32[]{:S(2)}, u32[]{:S(2)}) async-start(bf16[16,10,1,4096]{3,1,2,0:T(8,128)(2,1)} %bitcast_dynamic-update-slice_fusion), calls=%async_computation.13 | async-start | bytes 4194304 | tf_op jit(solution)/shard_map/all_to_all | solution.py:10
  870.2 46.7 %copy-start.14 = (bf16[160,16,1,2,128]{4,0,3,2,1:T(8,128)(2,1)S(1)}, bf16[160,16,1,2,128]{4,0,3,2,1:T(8,128)(2,1)}, u32[]{:S(2)}) copy-start(bf16[160,16,1,2,128]{4,0,3,2,1:T(8,128)(2,1)} %copy-done.13) | copy-start | bytes 3932164
  911.5 54.3 %all-to-all-start.9 = ((bf16[10,16,4096]{2,0,1:T(8,128)(2,1)}), bf16[10,16,4096]{2,0,1:T(8,128)(2,1)}, u32[]{:S(2)}, u32[]{:S(2)}) async-start(bf16[10,16,4096]{2,0,1:T(8,128)(2,1)} %copy.619), calls=%async_computation.9 | async-start | bytes 4194304 | tf_op jit(solution)/shard_map/all_to_all | solution.py:202
  965.8 54.0 %all-to-all-start.11 = ((bf16[10,16,4096]{2,0,1:T(8,128)(2,1)}), bf16[10,16,4096]{2,0,1:T(8,128)(2,1)}, u32[]{:S(2)}, u32[]{:S(2)}) async-start(bf16[10,16,4096]{2,0,1:T(8,128)(2,1)} %copy.624), calls=%async_computation.11 | async-start | bytes 4194304 | tf_op jit(solution)/shard_map/all_to_all | solution.py:203
  1024.3 3.1 copy-start.1
